TPU v7x, 128 devices: a whole 4x4x4 slice. The times are simulated.
128 devices in a mesh: dp: 32 (over y, z, core), expert: 4 (over x).
Axes of the slice: x: 4, y: 4, z: 4, core: 2. Of those that a mesh axis runs over, the one named last changes fastest.
Arguments:
- grad_parts: bfloat16 [32, 2048, 6144], P('dp', 'expert')
- bucket_order: int32 [256], replicated, may hold values from 0 to 255, each once
- master: float32 [4, 32, 16, 6144], P('expert', 'dp'), may hold values from -6 to 6
- first_moment: float32 [4, 32, 16, 6144], P('expert', 'dp'), may hold values from -0.6 to 0.6
- second_moment: float32 [4, 32, 16, 6144], P('expert', 'dp'), may hold values from 0.01 to 1
- step_count: int32 [4, 32, 16], P('expert', 'dp'), may hold values from 1 to 8
- max_rms: float32 [1], replicated, may hold values from 0.3 to 1
Outputs:
- new_master: float32 [4, 32, 16, 6144], P('expert', 'dp')
- new_first: float32 [4, 32, 16, 6144], P('expert', 'dp')
- new_second: float32 [4, 32, 16, 6144], P('expert', 'dp')
- new_params: bfloat16 [2048, 6144], P('expert')
Inputs may be any that keep to these rules, and one draw needn't show every extreme that they name: bucket_order is a permutation of the 256 buckets.
All inputs are finite; a program needn't handle non-finite values.
Results may differ from a plain program's by a relative error of at most 0.0085.
Values may be sent and summed in bfloat16 or wider, within the bound.
A program may use at most 128 MiB of HBM per device.

v0:
```python
import jax
import jax.numpy as jnp
from jax import lax
from jax.sharding import Mesh
from jax.sharding import PartitionSpec as P

DP = ("dp_0", "dp_1", "dp_2")
DP_EXPERT = ("dp_0", "dp_1", "dp_2", "expert")


def by_axis(shard, axes):
    for axis in axes:
        shard = lax.psum(shard, axis)
    return shard


def shards(grad_parts, bucket_order, master, first_moment, second_moment, step_count, max_rms):
    dp_count = lax.axis_size(DP)
    local_grad = grad_parts[0]
    rows_dev, row_width = local_grad.shape
    bucket_count = bucket_order.shape[0]
    bucket_rows = rows_dev // bucket_count
    owner_rows = rows_dev // dp_count
    buckets = local_grad.reshape(bucket_count, bucket_rows, row_width)
    slotted = jnp.take(buckets, bucket_order, axis=0)
    pieces = slotted.reshape(dp_count, owner_rows, row_width)
    received = lax.all_to_all(pieces, DP, split_axis=0, concat_axis=0, tiled=True)
    owned_sum = jnp.sum(received.astype(jnp.float32), axis=0)
    square_sum = by_axis(jnp.sum(owned_sum * owned_sum), DP_EXPERT)
    entries = float(rows_dev * row_width * lax.axis_size("expert"))
    clip_factor = jnp.minimum(1.0, max_rms[0] / jnp.sqrt(square_sum / entries + 1e-06))
    clipped = clip_factor * owned_sum
    new_first = 0.9 * first_moment[0, 0] + 0.1 * clipped
    new_second = 0.95 * second_moment[0, 0] + 0.05 * clipped * clipped
    step_float = step_count[0, 0].astype(jnp.float32)[:, None]
    first_fix = 1.0 - jnp.power(jnp.float32(0.9), step_float)
    second_fix = 1.0 - jnp.power(jnp.float32(0.95), step_float)
    ratio = new_first / first_fix / (jnp.sqrt(new_second / second_fix) + 1e-08)
    old_master = master[0, 0]
    new_master = old_master - 0.1 * (ratio + 0.1 * old_master)
    fresh = new_master.astype(jnp.bfloat16)
    gathered = lax.all_gather(fresh, DP, axis=0, tiled=True)
    slot_rows = gathered.reshape(bucket_count, bucket_rows, row_width)
    placed = jnp.zeros_like(slot_rows).at[bucket_order].set(slot_rows)
    return (
        new_master[None, None],
        new_first[None, None],
        new_second[None, None],
        placed.reshape(rows_dev, row_width),
    )


def solution(mesh):
    finer = Mesh(
        mesh.devices.reshape(4, 4, 2, mesh.shape["expert"]), ("dp_0", "dp_1", "dp_2", "expert")
    )
    return jax.shard_map(
        shards,
        mesh=finer,
        in_specs=(
            P(DP, "expert", None),
            P(),
            P("expert", DP, None, None),
            P("expert", DP, None, None),
            P("expert", DP, None, None),
            P("expert", DP, None),
            P(),
        ),
        out_specs=(
            P("expert", DP, None, None),
            P("expert", DP, None, None),
            P("expert", DP, None, None),
            P("expert", None),
        ),
        check_vma=False,
    )
```

profile of v0, /device:TPU:1, one launch (start us, length us, event | category | flops | bytes accessed | tf_op | source)
XLA Modules:
  0.0 324.8 jit_solution(6990627226799949666)
XLA Ops:
  7.2 0.0 all-gather.2.cloned.1.call-start
  7.2 0.7 compare_and_fusion
  7.9 0.7 compare_select_fusion
  8.6 0.1 broadcast_in_dim.26
  8.7 0.1 copy.11
  8.8 0.1 copy.12
  8.9 12.8 %reshape_squeeze.3 = bf16[256,2,6144]{2,1,0:T(2,128)(2,1)} reshape(bf16[1,512,6144]{2,1,0:T(8,128)(2,1)} %param.7) | data formatting | bytes 12582912 | tf_op jit(solution)/shard_map/reshape;squeeze | solution.py:24
  21.7 21.4 %gather_fusion = bf16[256,2,6144]{2,1,0:T(2,128)(2,1)} fusion(bf16[256,2,6144]{2,1,0:T(2,128)(2,1)} %reshape_squeeze.3, s32[1024]{0:T(1024)S(1)} %pad_clamp_fusion), kind=kCustom, calls=%fused_computation | custom fusion | bytes 12583936 | tf_op jit(solution)/shard_map/jit(_take)/gather | solution.py:25
  43.1 13.3 %gather.7 = bf16[32,16,6144]{2,1,0:T(8,128)(2,1)} reshape(bf16[256,2,6144]{2,1,0:T(2,128)(2,1)} %gather_fusion) | data formatting | bytes 12582912 | tf_op jit(solution)/shard_map/jit(_take)/gather | solution.py:25
  56.4 3.4 %broadcast_select_fusion = bf16[32,16,6144]{2,1,0:T(8,128)(2,1)S(1)} fusion(bf16[32,16,6144]{2,1,0:T(8,128)(2,1)} %gather.7, pred[32,16]{1,0:T(8,128)(4,1)S(1)} %copy.12), kind=kLoop, calls=%fused_computation.3 | loop fusion | flops 3145728 | bytes 12583424 | tf_op jit(solution)/shard_map/jit(_take)/select_n | solution.py:25
  59.9 82.5 %all_to_all.5 = bf16[32,16,6144]{2,1,0:T(8,128)(2,1)S(1)} all-to-all(bf16[32,16,6144]{2,1,0:T(8,128)(2,1)S(1)} %broadcast_select_fusion), channel_id=1, replica_groups=mesh['dp_0'=4,'dp_1'=4,'dp_2'=2,'expert'=4] {'dp_0','dp_1','dp_2'}, dimensions={0} | all-to-all | bytes 12582912 | tf_op jit(solution)/shard_map/all_to_all | solution.py:27
  142.4 0.0 copy-start.3
  142.4 0.0 copy-start
  142.4 0.0 copy-start.1
  142.4 1.0 convert_reduce_fusion
  143.4 0.7 multiply_reduce_fusion
  144.1 7.3 %psum.28 = f32[]{:T(128)} all-reduce(f32[]{:T(128)} %multiply_reduce_fusion), channel_id=1, replica_groups=mesh['dp_0'=4,'dp_1'=4,'dp_2'=2,'expert'=4] {'dp_0'}, use_global_device_ids=true, to_apply=%region_2.3 | all-reduce | flops 1 | bytes 8 | tf_op jit(solution)/shard_map/psum | solution.py:13
  151.5 8.0 %psum.29 = f32[]{:T(128)} all-reduce(f32[]{:T(128)} %psum.28), channel_id=1, replica_groups=mesh['dp_0'=4,'dp_1'=4,'dp_2'=2,'expert'=4] {'dp_1'}, use_global_device_ids=true, to_apply=%region_3.4 | all-reduce | flops 1 | bytes 8 | tf_op jit(solution)/shard_map/psum | solution.py:13
  159.4 0.0 copy-done.3
  159.4 7.0 %psum.30 = f32[]{:T(128)} all-reduce(f32[]{:T(128)} %psum.29), channel_id=1, replica_groups=mesh['dp_0'=4,'dp_1'=4,'dp_2'=2,'expert'=4] {'dp_2'}, use_global_device_ids=true, to_apply=%region_4.5 | all-reduce | flops 1 | bytes 8 | tf_op jit(solution)/shard_map/psum | solution.py:13
  167.0 9.3 %psum.31 = f32[]{:T(128)} all-reduce(f32[]{:T(128)} %psum.30), channel_id=1, replica_groups=mesh['dp_0'=4,'dp_1'=4,'dp_2'=2,'expert'=4] {'expert'}, use_global_device_ids=true, to_apply=%region_5.6 | all-reduce | flops 1 | bytes 8 | tf_op jit(solution)/shard_map/psum | solution.py:13
  177.0 0.0 copy-done
  177.0 0.0 copy-done.1
  177.0 0.0 copy-done.2
  177.1 1.0 fusion.9
  178.1 0.0 all-gather.2.cloned.1.call-update
  178.1 1.2 multiply_subtract_fusion
  179.3 45.1 %all-gather.2.cloned.1.call-done = bf16[512,6144]{1,0:T(8,128)(2,1)} async-done(((bf16[16,6144]{1,0:T(8,128)(2,1)}), bf16[512,6144]{1,0:T(8,128)(2,1)}) %all-gather.2.cloned.1.call-update) | async-done | bytes 6291472 | tf_op jit(solution)/shard_map/all_gather | solution.py:42
  224.4 12.8 %reshape.105 = bf16[256,2,6144]{2,1,0:T(2,128)(2,1)} reshape(bf16[512,6144]{1,0:T(8,128)(2,1)} %all-gather.2.cloned.1.call-done) | data formatting | bytes 12582912 | tf_op jit(solution)/shard_map/reshape | solution.py:43
  237.2 5.9 %broadcast_in_dim.32 = bf16[256,2,6144]{2,1,0:T(2,128)(2,1)} broadcast(bf16[]{:T(256)} %constant.13.clone.1), dimensions={} | broadcast | bytes 6291458 | tf_op jit(solution)/shard_map/broadcast_in_dim | solution.py:44
  243.1 61.6 %scatter_fusion = bf16[256,2,6144]{2,1,0:T(2,128)(2,1)} fusion(bf16[256,2,6144]{2,1,0:T(2,128)(2,1)} %broadcast_in_dim.32, s32[256]{0:T(256)S(1)} %compare_select_fusion, bf16[256,2,6144]{2,1,0:T(2,128)(2,1)} %reshape.105), kind=kCustom, calls=%fused_computation.1 | custom fusion | bytes 18875392 | tf_op jit(solution)/shard_map/scatter | solution.py:44
  304.7 13.3 %reshape.92 = bf16[512,6144]{1,0:T(8,128)(2,1)} reshape(bf16[256,2,6144]{2,1,0:T(2,128)(2,1)} %scatter_fusion) | data formatting | bytes 12582912 | tf_op jit(solution)/shard_map/reshape | solution.py:49
  (5 shorter events, 0.0 us)
Async XLA Ops:
  7.2 217.2 %all-gather.2.cloned.1.call-start = ((), (), s32[]{:S(2)}) async-start(), calls=%async_computation.1 | async-start | bytes 6488064 | tf_op jit(solution)/shard_map/all_gather | solution.py:42
  142.4 17.0 %copy-start.3 = (s32[1,1,16]{2,1,0:T(1,128)S(1)}, s32[1,1,16]{2,1,0:T(1,128)}, u32[]{:S(2)}) copy-start(s32[1,1,16]{2,1,0:T(1,128)} %param.12) | copy-start | bytes 196
  142.4 34.6 %copy-start = (f32[1,1,16,6144]{3,2,1,0:T(8,128)S(1)}, f32[1,1,16,6144]{3,2,1,0:T(8,128)}, u32[]{:S(2)}) copy-start(f32[1,1,16,6144]{3,2,1,0:T(8,128)} %param.9) | copy-start | bytes 1179652
  142.4 34.7 %copy-start.1 = (f32[1,1,16,6144]{3,2,1,0:T(8,128)S(1)}, f32[1,1,16,6144]{3,2,1,0:T(8,128)}, u32[]{:S(2)}) copy-start(f32[1,1,16,6144]{3,2,1,0:T(8,128)} %param.11) | copy-start | bytes 1179652
  142.4 34.7 %copy-start.2 = (f32[1,1,16,6144]{3,2,1,0:T(8,128)S(1)}, f32[1,1,16,6144]{3,2,1,0:T(8,128)}, u32[]{:S(2)}) copy-start(f32[1,1,16,6144]{3,2,1,0:T(8,128)} %param.10) | copy-start | bytes 1179652
Sparse Core Ops, SparseCore 0:
  178.2 46.1 all-gather.1
where the time goes:
time: 327 us; the launch traced here: 325 us
  local copies, waits for them, and re-layouts  141 us (43%)
  blocking collectives  114 us (35%)
  waiting for transfers between devices  45.1 us (14%)
  between operations  15.4 us (5%)
  other arithmetic  8.79 us (3%)
    all_to_all x1, blocking collectives, shards(): lax.all_to_all(pieces, DP, split_axis=0, concat_axis=0, tiled=True)  82.5 us
    scatter x1, local copies, waits for them, and re-layouts, shards(): placed = jnp.zeros_like(slot_rows).at[bucket_order].set(slot_rows)  61.6 us
    all_gather x1, waiting for transfers between devices, shards(): gathered = lax.all_gather(fresh, DP, axis=0, tiled=True)  45.1 us
    gather x2, local copies, waits for them, and re-layouts, shards(): slotted = jnp.take(buckets, bucket_order, axis=0)  34.7 us
    psum x4, blocking collectives, by_axis(): shard = lax.psum(shard, axis)  31.5 us
    reshape x1, local copies, waits for them, and re-layouts, shards(): placed.reshape(rows_dev, row_width)  13.3 us
    another operation x1, local copies, waits for them, and re-layouts, shards(): buckets = local_grad.reshape(bucket_count, bucket_rows, row_width)  12.8 us
    reshape x1, local copies, waits for them, and re-layouts, shards(): slot_rows = gathered.reshape(bucket_count, bucket_rows, row_width)  12.8 us
  transfers between devices with their start and end apart: 1, of which 1 were waited for; matrix products, arithmetic and copies ran while one was open for 0% of the time, Pallas kernels for 0%

commit v1 on v0

v1 whole, which is shorter than its diff:
```python
import functools

import jax
import jax.numpy as jnp
from jax import lax
from jax.experimental import pallas as pl
from jax.experimental.pallas import tpu as pltpu
from jax.sharding import Mesh
from jax.sharding import PartitionSpec as P

MESH = pl.DeviceIdType.MESH
BF16, F32 = jnp.bfloat16, jnp.float32
N = 4
WR = 512
WG = 1024
TILE = 256


def away(axis, by, n=N):
    return lax.rem(lax.axis_index(axis) + by, n)


def main_kernel(
    sizes, order, steps, max_rms, grad, master, first, second,
    out, new_master, new_first, new_second,
    own, sib, sb, hop, fin, s2, r2, tot, gsum, slots, perm, perm_t, st, fix, sq, s1, s2nd,
    load_sem, pair_sem, hop_sem, fin_sem, r2_sem, tot_sem, st_sem, x_sem, yz_sem, p1_sem, p2_sem, fwd_sem, half_sem,
):
    rows, width, nr, ng, entries = sizes
    my, mz, mc, mx = (lax.axis_index(a) for a in "yzcx")
    half = width // 2
    coords = {"y": my, "z": mz}

    def axes(block):
        return ("y", "z") if block % 2 == 0 else ("z", "y")

    def remote(src, dst, sems, at, where):
        return pltpu.make_async_remote_copy(
            src_ref=src, dst_ref=dst, send_sem=sems.at[(0, *at)], recv_sem=sems.at[(1, *at)],
            device_id=where, device_id_type=MESH,
        )

    sent = []

    def start(copies):
        for c in copies:
            c.start()
        sent.extend(copies)
        return copies

    def arrived(copies):
        for c in copies:
            c.wait_recv()

    def load(k):
        cols = pl.ds(pl.multiple_of(mc * half + k * WR, WR), WR)
        return pltpu.make_async_copy(grad.at[0, :, cols], own.at[k], load_sem.at[k])

    loads = [load(k) for k in range(nr)]
    states = [
        pltpu.make_async_copy(a.at[0, 0], st.at[i], st_sem.at[i])
        for i, a in enumerate((master, first, second))
    ]
    for c in loads:
        c.start()
    for c in states:
        c.start()

    sibling = {"c": 1 - mc}
    group_x = [(i, j) for i in range(N) for j in range(2) if i or j]
    group_yz = [(i, j) for i in range(N) for j in range(N) if i or j]
    peers_x = [{"x": away("x", i), "c": away("c", j, 2)} for i, j in group_x]
    peers_yz = [{"y": away("y", i), "z": away("z", j)} for i, j in group_yz]
    barrier = pltpu.get_barrier_semaphore()
    for peer in [*peers_x, *peers_yz]:
        pl.semaphore_signal(barrier, inc=1, device_id=peer, device_id_type=MESH)

    def fill(t, _):
        i = lax.broadcasted_iota(jnp.int32, (16, rows), 0)
        picked = jnp.zeros((16, rows), jnp.int32)
        for b in range(8):
            picked = jnp.where(i // 2 == b, order[t * 8 + b] * 2, picked)
        hit = lax.broadcasted_iota(jnp.int32, (16, rows), 1) == picked + i % 2
        perm[pl.ds(pl.multiple_of(t * 16, 16), 16), :] = jnp.where(hit, 1.0, 0.0).astype(BF16)
        return 0

    lax.fori_loop(0, rows // 16, fill, 0)
    pl.semaphore_wait(barrier, len(peers_x) + len(peers_yz))

    def pair(k):
        cols = pl.ds(pl.multiple_of((1 - mc) * half + k * WR, WR), WR)
        return remote(grad.at[0, :, cols], sib.at[k], pair_sem, (k,), sibling)

    pairs = start([pair(k) for k in range(nr)])

    def pick_rows(k):
        loads[k].wait()
        arrived([pairs[k]])
        for t in range(WR // TILE):
            cols = pl.ds(t * TILE, TILE)
            both = own[k, :, cols].astype(F32) + sib[k, :, cols].astype(F32)
            moved = jnp.dot(perm[...], both.astype(BF16), preferred_element_type=F32)
            moved = moved.astype(BF16).reshape(N, N, 32, TILE)
            for i in range(N):
                for j in range(N):
                    at = (i, j) if k % 2 == 0 else (j, i)
                    sb[k, at[0], at[1], :, cols] = moved[i, j]

    def beside(axis):
        return coords[axis], away(axis, 1), away(axis, 2), away(axis, 3)

    lo, hi = pl.ds(0, 2), pl.ds(2, 2)

    def first_hops(k):
        a = axes(k)[0]
        _, up, far, down = beside(a)
        hops = [
            remote(sb.at[k, far, lo], hop.at[k, 0], hop_sem, (k, 0), {a: up}),
            remote(sb.at[k, far, hi], hop.at[k, 1], hop_sem, (k, 1), {a: down}),
        ]
        plain = [
            remote(sb.at[k, up, hi], fin.at[k, 0, hi], fin_sem, (k, 0), {a: up}),
            remote(sb.at[k, down, lo], fin.at[k, 1, lo], fin_sem, (k, 1), {a: down}),
        ]
        return start(hops), start(plain)

    def add_into(k, to, j0, slot):
        def body(i, _):
            j, r = i // 2, pl.ds(pl.multiple_of((i % 2) * 16, 16), 16)
            total = sb[k, to, j0 + j, r, :].astype(F32) + hop[k, slot, j, r, :].astype(F32)
            sb[k, to, j0 + j, r, :] = total.astype(BF16)
            return 0

        lax.fori_loop(0, 4, body, 0)

    def second_hops(k, hops):
        a = axes(k)[0]
        _, up, _, down = beside(a)
        arrived([hops[0]])
        add_into(k, up, 0, 0)
        one = remote(sb.at[k, up, lo], fin.at[k, 0, lo], fin_sem, (k, 2), {a: up})
        start([one])
        arrived([hops[1]])
        add_into(k, down, 2, 1)
        two = remote(sb.at[k, down, hi], fin.at[k, 1, hi], fin_sem, (k, 3), {a: down})
        start([two])
        return [one, two]

    def sum3(k, me, j, r):
        return sb[k, me, j, r, :].astype(F32) + fin[k, 0, j, r, :].astype(F32) + fin[k, 1, j, r, :].astype(F32)

    def across(k, waits):
        a, b = axes(k)
        me = coords[a]
        arrived(waits)
        copies = []
        for d in (2, 1, 3):
            j = away(b, d)

            def body(i, _, j=j, d=d):
                r = pl.ds(pl.multiple_of(i * 16, 16), 16)
                s2[k, d - 1, r, :] = sum3(k, me, j, r).astype(BF16)
                return 0

            lax.fori_loop(0, 2, body, 0)
            copies += start([remote(s2.at[k, d - 1], r2.at[k, d - 1], r2_sem, (k, d - 1), {b: j})])
        return copies

    def finish(k, waits):
        a, b = axes(k)
        me, mj = coords[a], coords[b]
        arrived(waits)
        cols = pl.ds(pl.multiple_of(mc * half + k * WR, WR), WR)
        for i in range(2):
            r = pl.ds(i * 16, 16)
            total = sum3(k, me, mj, r)
            for d in range(3):
                total = total + r2[k, d, r, :].astype(F32)
            tot[k, i] = total
            square = total * total
            folded = square[:, :128]
            for t in range(1, WR // 128):
                folded = folded + square[:, t * 128 : (t + 1) * 128]
            sq[...] += folded[:8] + folded[8:]
        gsum[:, cols] = tot[k, mc]
        return start([remote(tot.at[k, 1 - mc], gsum.at[:, cols], tot_sem, (k,), sibling)])

    sq[...] = jnp.zeros_like(sq)
    hops, plain, second_half, sums, shared = {}, {}, {}, {}, []
    for t in range(nr + 3):
        if t < nr:
            pick_rows(t)
            hops[t], plain[t] = first_hops(t)
        if 0 <= t - 1 < nr:
            second_half[t - 1] = second_hops(t - 1, hops[t - 1])
        if 0 <= t - 2 < nr:
            sums[t - 2] = across(t - 2, plain[t - 2] + second_half[t - 2])
        if 0 <= t - 3 < nr:
            shared += finish(t - 3, sums[t - 3])

    mine_x, mine_yz = mx * 2 + mc, my * N + mz
    s1[mine_x] = sq[...]
    across_x = start([
        remote(sq, s1.at[mine_x], x_sem, (n,), peer) for n, peer in enumerate(peers_x)
    ])

    def flip(t, _):
        r = pl.ds(pl.multiple_of(t * 128, 128), 128)
        i = lax.broadcasted_iota(jnp.int32, (128, rows), 0) + t * 128
        eye = jnp.where(i == lax.broadcasted_iota(jnp.int32, (128, rows), 1), 1.0, 0.0).astype(BF16)
        perm_t[r, :] = lax.dot_general(
            eye, perm[...], (((1,), (1,)), ((), ())), preferred_element_type=F32
        ).astype(BF16)
        return 0

    lax.fori_loop(0, rows // 128, flip, 0)
    lane_row = lax.broadcasted_iota(jnp.int32, (16, 128), 0)
    count = jnp.zeros((16, 128), jnp.int32)
    for i in range(16):
        count = jnp.where(lane_row == i, steps[0, 0, i], count)
    count = count.astype(F32)
    fix[0] = 1.0 - jnp.power(jnp.full((16, 128), 0.9, F32), count)
    fix[1] = 1.0 - jnp.power(jnp.full((16, 128), 0.95, F32), count)
    for c in states:
        c.wait()

    arrived(across_x)
    part = s1[0]
    for i in range(1, 2 * N):
        part = part + s1[i]
    s2nd[mine_yz] = part
    mine = s2nd.at[mine_yz]
    across_yz = start([remote(mine, mine, yz_sem, (n,), peer) for n, peer in enumerate(peers_yz)])
    arrived(shared)
    arrived(across_yz)
    part = s2nd[0]
    for i in range(1, N * N):
        part = part + s2nd[i]
    square_sum = jnp.sum(jnp.sum(part, axis=1, keepdims=True), axis=0, keepdims=True)
    clip = jnp.minimum(1.0, max_rms[0] / jnp.sqrt(square_sum / entries + 1e-06))

    def update(k):
        def body(t, _):
            cols = pl.ds(pl.multiple_of(k * WG + t * 128, 128), 128)
            clipped = clip * gsum[:, cols]
            moment = 0.9 * st[1, :, cols] + 0.1 * clipped
            variance = 0.95 * st[2, :, cols] + 0.05 * clipped * clipped
            ratio = moment / fix[0] / (jnp.sqrt(variance / fix[1]) + 1e-08)
            old = st[0, :, cols]
            fresh = old - 0.1 * (ratio + 0.1 * old)
            new_master[0, 0, :, cols] = fresh
            new_first[0, 0, :, cols] = moment
            new_second[0, 0, :, cols] = variance
            slots[my, mz, mc, :, cols] = fresh.astype(BF16)
            return 0

        lax.fori_loop(0, WG // 128, body, 0)
        cols = pl.ds(k * WG, WG)
        a = axes(k)[0]
        mine = slots.at[my, mz, mc, :, cols]
        return start([remote(mine, mine, p1_sem, (k, d - 1), {a: away(a, d)}) for d in (2, 1, 3)])

    def row(k, at, part):
        cols = pl.ds(k * WG, WG)
        if k % 2 == 0:
            return slots.at[part, at, mc, :, cols]
        return slots.at[at, part, mc, :, cols]

    def spread(k, waits):
        arrived(waits)
        b = axes(k)[1]
        me, up, _, down = beside(b)
        mine = row(k, me, pl.ds(0, N))
        return start([
            remote(mine, mine, p2_sem, (k, 0), {b: up}),
            remote(mine, mine, p2_sem, (k, 1), {b: down}),
        ])

    def forward(k, waits):
        b = axes(k)[1]
        _, up, _, down = beside(b)
        arrived(waits[:1])
        one, two = row(k, down, lo), row(k, up, hi)
        copies = start([remote(one, one, fwd_sem, (k, 0), {b: up})])
        arrived(waits[1:])
        return copies + start([remote(two, two, fwd_sem, (k, 1), {b: down})])

    def to_sibling(k, waits):
        arrived(waits)
        block = slots.at[:, :, mc, :, pl.ds(k * WG, WG)]
        return start([remote(block, block, half_sem, (k,), sibling)])

    def put_back(k, waits):
        arrived(waits)
        for t in range(WG // TILE):
            cols = pl.ds(k * WG + t * TILE, TILE)
            block = slots[:, :, :, :, cols].reshape(rows, TILE)
            out[:, cols] = jnp.dot(perm_t[...], block, preferred_element_type=F32).astype(BF16)

    ups = [update(k) for k in range(ng)]
    across_b, forwards, halves = {}, {}, {}
    for t in range(ng + 3):
        if t < ng:
            across_b[t] = spread(t, ups[t])
        if 0 <= t - 1 < ng:
            forwards[t - 1] = forward(t - 1, across_b[t - 1])
        if 0 <= t - 2 < ng:
            halves[t - 2] = to_sibling(t - 2, forwards[t - 2])
        if 0 <= t - 3 < ng:
            put_back(t - 3, halves[t - 3])
    for c in sent:
        c.wait_send()


def write_kernel(*refs):
    n = (len(refs) - 1) // 2
    copies = [
        pltpu.make_async_copy(refs[i], refs[n + i], refs[2 * n].at[i]) for i in range(n)
    ]
    for c in copies:
        c.start()
    for c in copies:
        c.wait()


def shards(grad_parts, bucket_order, master, first_moment, second_moment, step_count, max_rms):
    _, rows, width = grad_parts.shape
    own_rows = master.shape[2]
    nr, ng = width // 2 // WR, width // WG
    entries = float(rows * width * lax.axis_size("x"))
    dma = pltpu.SemaphoreType.DMA
    anywhere = pl.BlockSpec(memory_space=pl.ANY)
    smem = pl.BlockSpec(memory_space=pltpu.SMEM)
    vmem = pl.BlockSpec(memory_space=pltpu.VMEM)
    state = pltpu.VMEM(master.shape, F32)
    results = pl.pallas_call(
        functools.partial(main_kernel, (rows, width, nr, ng, entries)),
        out_shape=(pltpu.VMEM((rows, width), BF16), state, state, state),
        in_specs=[smem] * 3 + [pl.BlockSpec(memory_space=pltpu.HBM)] * 4,
        out_specs=[vmem] * 4,
        scratch_shapes=[
            pltpu.VMEM((nr, rows, WR), BF16),
            pltpu.VMEM((nr, rows, WR), BF16),
            pltpu.VMEM((nr, N, N, 32, WR), BF16),
            pltpu.VMEM((nr, 2, 2, 32, WR), BF16),
            pltpu.VMEM((nr, 2, N, 32, WR), BF16),
            pltpu.VMEM((nr, 3, 32, WR), BF16),
            pltpu.VMEM((nr, 3, 32, WR), BF16),
            pltpu.VMEM((nr, 2, 16, WR), F32),
            pltpu.VMEM((own_rows, width), F32),
            pltpu.VMEM((N, N, 2, own_rows, width), BF16),
            pltpu.VMEM((rows, rows), BF16),
            pltpu.VMEM((rows, rows), BF16),
            pltpu.VMEM((3, own_rows, width), F32),
            pltpu.VMEM((2, own_rows, 128), F32),
            pltpu.VMEM((8, 128), F32),
            pltpu.VMEM((2 * N, 8, 128), F32),
            pltpu.VMEM((N * N, 8, 128), F32),
            dma((nr,)),
            dma((2, nr)),
            dma((2, nr, 2)),
            dma((2, nr, 4)),
            dma((2, nr, 3)),
            dma((2, nr)),
            dma((3,)),
            dma((2, 7)),
            dma((2, 15)),
            dma((2, ng, 3)),
            dma((2, ng, 2)),
            dma((2, ng, 2)),
            dma((2, ng)),
        ],
        compiler_params=pltpu.CompilerParams(
            collective_id=0, has_side_effects=True, vmem_limit_bytes=48 << 20
        ),
    )(bucket_order, step_count, max_rms, grad_parts, master, first_moment, second_moment)
    fresh, *moved = pl.pallas_call(
        write_kernel,
        out_shape=[jax.ShapeDtypeStruct(r.shape, r.dtype) for r in results],
        in_specs=[anywhere] * 4,
        out_specs=[pl.BlockSpec(memory_space=pltpu.HBM)] * 4,
        scratch_shapes=[dma((4,))],
    )(*results)
    return (*moved, fresh)


def solution(mesh):
    dp = ("y", "z", "c")
    finer = Mesh(mesh.devices.reshape(N, N, 2, mesh.shape["expert"]), (*dp, "x"))
    state = P("x", dp, None, None)
    return jax.shard_map(
        shards,
        mesh=finer,
        in_specs=(P(dp, "x", None), P(), state, state, state, P("x", dp, None), P()),
        out_specs=(state, state, state, P("x", None)),
        check_vma=False,
    )
```

time: 327 us -> 314 us (0.960)
  Pallas kernels: 0 us -> 308 us
  local copies, waits for them, and re-layouts: 141 us -> 4.87 us
  blocking collectives: 114 us -> 0 us
  waiting for transfers between devices: 45.1 us -> 0 us
  between operations: 15.4 us -> 1.3 us
  other arithmetic: 8.79 us -> 0 us
    pallas_call x0 -> x2, Pallas kernels: none -> 308 us  [the longest x1 227 us: shards(): pl.pallas_call(write_kernel, out_shape=[jax.ShapeDtypeStruct(r.shape, r.d...]
    all_to_all x1 -> x0, blocking collectives: 82.5 us -> none  [shards(): lax.all_to_all(pieces, DP, split_axis=0, concat_axis=0, tiled=True)]
    scatter x1 -> x0, local copies, waits for them, and re-layouts: 61.6 us -> none  [shards(): placed = jnp.zeros_like(slot_rows).at[bucket_order].set(slot_rows)]
    all_gather x1 -> x0, waiting for transfers between devices: 45.1 us -> none  [shards(): gathered = lax.all_gather(fresh, DP, axis=0, tiled=True)]
    gather x2 -> x0, local copies, waits for them, and re-layouts: 34.7 us -> none  [shards(): slotted = jnp.take(buckets, bucket_order, axis=0)]
    psum x4 -> x0, blocking collectives: 31.5 us -> none  [by_axis(): shard = lax.psum(shard, axis)]
    reshape x2 -> x0, local copies, waits for them, and re-layouts: 26.1 us -> none  [the longest x1 13.3 us: shards(): placed.reshape(rows_dev, row_width)]
    another operation x1 -> x0, local copies, waits for them, and re-layouts: 12.8 us -> none  [shards(): buckets = local_grad.reshape(bucket_count, bucket_rows, row_width)]
  transfers between devices with their start and end apart: 1 -> 0, of which waited for: 1 -> 0; matrix products, arithmetic and copies ran while one was open for 0% -> 0% of each run, Pallas kernels for 0% -> 0%
where the time goes in v1:
time: 314 us
  Pallas kernels  308 us (98%)
  local copies, waits for them, and re-layouts  4.87 us (2%)
    pallas_call x1, Pallas kernels, shards(): pl.pallas_call(write_kernel, out_shape=[jax.ShapeDtypeStruct(r.shape, r.d...  227 us
    pallas_call x1, Pallas kernels, shards(): pl.pallas_call(functools.partial(main_kernel, (rows, width, nr, ng, entri...  80.1 us

profile of v1, /device:TPU:1, one launch (start us, length us, event | category | flops | bytes accessed | tf_op | source)
XLA Modules:
  0.0 313.8 jit_solution(12954297485211957670)
XLA Ops:
  1.3 80.1 %shard_map.102 = (bf16[512,6144]{1,0:T(8,128)(2,1)S(1)}, f32[1,1,16,6144]{3,2,1,0:T(8,128)S(1)}, f32[1,1,16,6144]{3,2,1,0:T(8,128)S(1)}, f32[1,1,16,6144]{3,2,1,0:T(8,128)S(1)}) custom-call(s32[256]{0:T(256)} %order.1, s32[1,1,16]{2,1,0:T(1,128)} %steps.1, f32[1]{0:T(128)S(6)} %copy.11.max_rms, bf16[1,512,6144]{2,1,0:T(8,128)(2,1)} %grad.1, ...), custom_call_target="tpu_custom_call" | custom-call | tf_op jit(solution)/shard_map/pallas_call | solution.py:336
  81.4 0.0 copy-start
  81.4 2.6 copy-done
  84.1 0.0 copy-start.1
  84.1 0.7 copy-done.1
  84.8 0.0 copy-start.2
  84.8 0.7 copy-done.2
  85.6 0.0 copy-start.3
  85.6 0.7 copy-done.3
  86.3 227.5 %shard_map.103 = (bf16[512,6144]{1,0:T(8,128)(2,1)}, f32[1,1,16,6144]{3,2,1,0:T(8,128)}, f32[1,1,16,6144]{3,2,1,0:T(8,128)}, f32[1,1,16,6144]{3,2,1,0:T(8,128)}) custom-call(bf16[512,6144]{1,0:T(8,128)(2,1)} %copy-done, f32[1,1,16,6144]{3,2,1,0:T(8,128)} %copy-done.1, f32[1,1,16,6144]{3,2,1,0:T(8,128)} %copy-done.2, f32[1,1,16,6144]{3,2,1,0:T(8,128)} %copy-done.3), custom_call_target="tpu_custom_call" | custom-call | tf_op jit(solution)/shard_map/pallas_call | solution.py:377
Async XLA Ops:
  81.4 2.6 copy-start
  84.1 0.7 copy-start.1
  84.8 0.7 copy-start.2
  85.6 0.7 copy-start.3

commit v2 on v1

--- a/solution.py
+++ b/solution.py
@@ -380,7 +380,8 @@
         in_specs=[anywhere] * 4,
         out_specs=[pl.BlockSpec(memory_space=pltpu.HBM)] * 4,
         scratch_shapes=[dma((4,))],
-    )(*results)
+        compiler_params=pltpu.CompilerParams(vmem_limit_bytes=1 << 20),
+    )(*(pltpu.with_memory_space_constraint(r, pltpu.VMEM) for r in results))
     return (*moved, fresh)
 
 

time: 314 us -> 84.7 us (0.27)
  Pallas kernels: 308 us -> 83.2 us
  local copies, waits for them, and re-layouts: 4.87 us -> 0 us
    pallas_call x1, Pallas kernels: 227 us -> 3.09 us  [shards(): pl.pallas_call(write_kernel, out_shape=[jax.ShapeDtypeStruct(r.shape, r.d...]
    unnamed x8 -> x0, local copies, waits for them, and re-layouts: 4.87 us -> none
where the time goes in v2:
time: 84.7 us; the launch traced here: 84.5 us
  Pallas kernels  83.2 us (98%)
  between operations  1.29 us (2%)
    pallas_call x1, Pallas kernels, shards(): pl.pallas_call(functools.partial(main_kernel, (rows, width, nr, ng, entri...  80.1 us
    pallas_call x1, Pallas kernels, shards(): pl.pallas_call(write_kernel, out_shape=[jax.ShapeDtypeStruct(r.shape, r.d...  3.09 us

profile of v2, /device:TPU:1, one launch (start us, length us, event | category | flops | bytes accessed | tf_op | source)
XLA Modules:
  0.0 84.5 jit_solution(11872637258162524645)
XLA Ops:
  1.3 80.1 %shard_map.102 = (bf16[512,6144]{1,0:T(8,128)(2,1)S(1)}, f32[1,1,16,6144]{3,2,1,0:T(8,128)S(1)}, f32[1,1,16,6144]{3,2,1,0:T(8,128)S(1)}, f32[1,1,16,6144]{3,2,1,0:T(8,128)S(1)}) custom-call(s32[256]{0:T(256)} %order.1, s32[1,1,16]{2,1,0:T(1,128)} %steps.1, f32[1]{0:T(128)S(6)} %copy.11.max_rms, bf16[1,512,6144]{2,1,0:T(8,128)(2,1)} %grad.1, ...), custom_call_target="tpu_custom_call" | custom-call | tf_op jit(solution)/shard_map/pallas_call | solution.py:336
  81.4 3.1 %shard_map.103 = (bf16[512,6144]{1,0:T(8,128)(2,1)}, f32[1,1,16,6144]{3,2,1,0:T(8,128)}, f32[1,1,16,6144]{3,2,1,0:T(8,128)}, f32[1,1,16,6144]{3,2,1,0:T(8,128)}) custom-call(bf16[512,6144]{1,0:T(8,128)(2,1)S(1)} %get-tuple-element.12.refs_0_, f32[1,1,16,6144]{3,2,1,0:T(8,128)S(1)} %get-tuple-element.13.refs_1_, ...), custom_call_target="tpu_custom_call" | custom-call | tf_op jit(solution)/shard_map/pallas_call | solution.py:377

commit v3 on v2

--- a/solution.py
+++ b/solution.py
@@ -14,6 +14,8 @@
 WR = 512
 WG = 1024
 TILE = 256
+RS_LAG = (6, 6, 6)
+AG_LAG = (6, 6, 1)
 
 
 def away(axis, by, n=N):
@@ -21,10 +23,10 @@
 
 
 def main_kernel(
-    sizes, order, steps, max_rms, grad, master, first, second,
+    sizes, order_in, steps_in, max_rms_in, grad, master, first, second,
     out, new_master, new_first, new_second,
-    own, sib, sb, hop, fin, s2, r2, tot, gsum, slots, perm, perm_t, st, fix, sq, s1, s2nd,
-    load_sem, pair_sem, hop_sem, fin_sem, r2_sem, tot_sem, st_sem, x_sem, yz_sem, p1_sem, p2_sem, fwd_sem, half_sem,
+    own, sib, sb, hop, fin, s2, r2, tot, gsum, slots, perm, perm_t, st, fix, sq, s1, s2nd, order, steps, max_rms,
+    load_sem, pair_sem, hop_sem, fin_sem, r2_sem, tot_sem, st_sem, x_sem, yz_sem, p1_sem, p2_sem, fwd_sem, half_sem, small_sem, met_sem,
 ):
     rows, width, nr, ng, entries = sizes
     my, mz, mc, mx = (lax.axis_index(a) for a in "yzcx")
@@ -61,9 +63,11 @@
         pltpu.make_async_copy(a.at[0, 0], st.at[i], st_sem.at[i])
         for i, a in enumerate((master, first, second))
     ]
-    for c in loads:
-        c.start()
-    for c in states:
+    small = [
+        pltpu.make_async_copy(a, b, small_sem.at[i])
+        for i, (a, b) in enumerate(((order_in, order), (steps_in, steps), (max_rms_in, max_rms)))
+    ]
+    for c in [*small, *loads, *states]:
         c.start()
 
     sibling = {"c": 1 - mc}
@@ -71,9 +75,14 @@
     group_yz = [(i, j) for i in range(N) for j in range(N) if i or j]
     peers_x = [{"x": away("x", i), "c": away("c", j, 2)} for i, j in group_x]
     peers_yz = [{"y": away("y", i), "z": away("z", j)} for i, j in group_yz]
+    def signal(sem, where):
+        pl.semaphore_signal(sem, inc=1, device_id=where, device_id_type=MESH)
+
+    beside_x = [{"x": away("x", 1)}, {"x": away("x", 3)}]
+    nearest = [sibling, *({a: away(a, d)} for a in "yz" for d in (1, 3)), *beside_x]
     barrier = pltpu.get_barrier_semaphore()
-    for peer in [*peers_x, *peers_yz]:
-        pl.semaphore_signal(barrier, inc=1, device_id=peer, device_id_type=MESH)
+    for peer in nearest:
+        signal(barrier, peer)
 
     def fill(t, _):
         i = lax.broadcasted_iota(jnp.int32, (16, rows), 0)
@@ -84,14 +93,17 @@
         perm[pl.ds(pl.multiple_of(t * 16, 16), 16), :] = jnp.where(hit, 1.0, 0.0).astype(BF16)
         return 0
 
+    small[0].wait()
     lax.fori_loop(0, rows // 16, fill, 0)
-    pl.semaphore_wait(barrier, len(peers_x) + len(peers_yz))
+    pl.semaphore_wait(barrier, len(nearest))
 
     def pair(k):
         cols = pl.ds(pl.multiple_of((1 - mc) * half + k * WR, WR), WR)
         return remote(grad.at[0, :, cols], sib.at[k], pair_sem, (k,), sibling)
 
     pairs = start([pair(k) for k in range(nr)])
+    for peer in beside_x:
+        signal(met_sem.at[0], peer)
 
     def pick_rows(k):
         loads[k].wait()
@@ -187,19 +199,27 @@
 
     sq[...] = jnp.zeros_like(sq)
     hops, plain, second_half, sums, shared = {}, {}, {}, {}, []
-    for t in range(nr + 3):
+    for t in range(nr + sum(RS_LAG)):
         if t < nr:
             pick_rows(t)
             hops[t], plain[t] = first_hops(t)
-        if 0 <= t - 1 < nr:
-            second_half[t - 1] = second_hops(t - 1, hops[t - 1])
-        if 0 <= t - 2 < nr:
-            sums[t - 2] = across(t - 2, plain[t - 2] + second_half[t - 2])
-        if 0 <= t - 3 < nr:
-            shared += finish(t - 3, sums[t - 3])
+        k = t - RS_LAG[0]
+        if 0 <= k < nr:
+            second_half[k] = second_hops(k, hops[k])
+        k -= RS_LAG[1]
+        if k == 0:
+            pl.semaphore_wait(met_sem.at[0], 2)
+            for peer in beside_x:
+                signal(met_sem.at[1], peer)
+        if 0 <= k < nr:
+            sums[k] = across(k, plain[k] + second_half[k])
+        k -= RS_LAG[2]
+        if 0 <= k < nr:
+            shared += finish(k, sums[k])
 
     mine_x, mine_yz = mx * 2 + mc, my * N + mz
     s1[mine_x] = sq[...]
+    pl.semaphore_wait(met_sem.at[1], 2)
     across_x = start([
         remote(sq, s1.at[mine_x], x_sem, (n,), peer) for n, peer in enumerate(peers_x)
     ])
@@ -214,6 +234,8 @@
         return 0
 
     lax.fori_loop(0, rows // 128, flip, 0)
+    small[1].wait()
+    small[2].wait()
     lane_row = lax.broadcasted_iota(jnp.int32, (16, 128), 0)
     count = jnp.zeros((16, 128), jnp.int32)
     for i in range(16):
@@ -299,23 +321,31 @@
 
     ups = [update(k) for k in range(ng)]
     across_b, forwards, halves = {}, {}, {}
-    for t in range(ng + 3):
+    for t in range(ng + sum(AG_LAG)):
         if t < ng:
             across_b[t] = spread(t, ups[t])
-        if 0 <= t - 1 < ng:
-            forwards[t - 1] = forward(t - 1, across_b[t - 1])
-        if 0 <= t - 2 < ng:
-            halves[t - 2] = to_sibling(t - 2, forwards[t - 2])
-        if 0 <= t - 3 < ng:
-            put_back(t - 3, halves[t - 3])
+        k = t - AG_LAG[0]
+        if 0 <= k < ng:
+            forwards[k] = forward(k, across_b[k])
+        k -= AG_LAG[1]
+        if 0 <= k < ng:
+            halves[k] = to_sibling(k, forwards[k])
+        k -= AG_LAG[2]
+        if 0 <= k < ng:
+            put_back(k, halves[k])
     for c in sent:
         c.wait_send()
 
 
 def write_kernel(*refs):
     n = (len(refs) - 1) // 2
+    sem = refs[2 * n]
     copies = [
-        pltpu.make_async_copy(refs[i], refs[n + i], refs[2 * n].at[i]) for i in range(n)
+        pltpu.make_async_copy(refs[0].at[pl.ds(i * 64, 64)], refs[n].at[pl.ds(i * 64, 64)], sem.at[i])
+        for i in range(8)
+    ]
+    copies += [
+        pltpu.make_async_copy(refs[i], refs[n + i], sem.at[7 + i]) for i in range(1, n)
     ]
     for c in copies:
         c.start()
@@ -330,13 +360,12 @@
     entries = float(rows * width * lax.axis_size("x"))
     dma = pltpu.SemaphoreType.DMA
     anywhere = pl.BlockSpec(memory_space=pl.ANY)
-    smem = pl.BlockSpec(memory_space=pltpu.SMEM)
     vmem = pl.BlockSpec(memory_space=pltpu.VMEM)
     state = pltpu.VMEM(master.shape, F32)
     results = pl.pallas_call(
         functools.partial(main_kernel, (rows, width, nr, ng, entries)),
         out_shape=(pltpu.VMEM((rows, width), BF16), state, state, state),
-        in_specs=[smem] * 3 + [pl.BlockSpec(memory_space=pltpu.HBM)] * 4,
+        in_specs=[pl.BlockSpec(memory_space=pltpu.HBM)] * 7,
         out_specs=[vmem] * 4,
         scratch_shapes=[
             pltpu.VMEM((nr, rows, WR), BF16),
@@ -356,6 +385,9 @@
             pltpu.VMEM((8, 128), F32),
             pltpu.VMEM((2 * N, 8, 128), F32),
             pltpu.VMEM((N * N, 8, 128), F32),
+            pltpu.SMEM(bucket_order.shape, jnp.int32),
+            pltpu.SMEM(step_count.shape, jnp.int32),
+            pltpu.SMEM(max_rms.shape, F32),
             dma((nr,)),
             dma((2, nr)),
             dma((2, nr, 2)),
@@ -369,6 +401,8 @@
             dma((2, ng, 2)),
             dma((2, ng, 2)),
             dma((2, ng)),
+            dma((3,)),
+            pltpu.SemaphoreType.REGULAR((2,)),
         ],
         compiler_params=pltpu.CompilerParams(
             collective_id=0, has_side_effects=True, vmem_limit_bytes=48 << 20
@@ -379,7 +413,7 @@
         out_shape=[jax.ShapeDtypeStruct(r.shape, r.dtype) for r in results],
         in_specs=[anywhere] * 4,
         out_specs=[pl.BlockSpec(memory_space=pltpu.HBM)] * 4,
-        scratch_shapes=[dma((4,))],
+        scratch_shapes=[dma((11,))],
         compiler_params=pltpu.CompilerParams(vmem_limit_bytes=1 << 20),
     )(*(pltpu.with_memory_space_constraint(r, pltpu.VMEM) for r in results))
     return (*moved, fresh)

time: 84.7 us -> 71.6 us (0.85)
  Pallas kernels: 83.2 us -> 70.2 us
    pallas_call x1, Pallas kernels: 80.1 us -> 67.1 us  [shards(): pl.pallas_call(functools.partial(main_kernel, (rows, width, nr, ng, entri...]
where the time goes in v3:
time: 71.6 us; the launch traced here: 71.5 us
  Pallas kernels  70.2 us (98%)
  between operations  1.29 us (2%)
    pallas_call x1, Pallas kernels, shards(): pl.pallas_call(functools.partial(main_kernel, (rows, width, nr, ng, entri...  67.1 us
    pallas_call x1, Pallas kernels, shards(): pl.pallas_call(write_kernel, out_shape=[jax.ShapeDtypeStruct(r.shape, r.d...  3.11 us

profile of v3, /device:TPU:1, one launch (start us, length us, event | category | flops | bytes accessed | tf_op | source)
XLA Modules:
  0.0 71.5 jit_solution(3046894568482158446)
XLA Ops:
  1.3 67.1 %shard_map.102 = (bf16[512,6144]{1,0:T(8,128)(2,1)S(1)}, f32[1,1,16,6144]{3,2,1,0:T(8,128)S(1)}, f32[1,1,16,6144]{3,2,1,0:T(8,128)S(1)}, f32[1,1,16,6144]{3,2,1,0:T(8,128)S(1)}) custom-call(s32[256]{0:T(256)} %order_in.1, s32[1,1,16]{2,1,0:T(1,128)} %steps_in.1, f32[1]{0:T(128)S(6)} %copy.11.max_rms_in, bf16[1,512,6144]{2,1,0:T(8,128)(2,1)} %grad.1, ...), custom_call_target="tpu_custom_call" | custom-call | tf_op jit(solution)/shard_map/pallas_call | solution.py:365
  68.4 3.1 %shard_map.103 = (bf16[512,6144]{1,0:T(8,128)(2,1)}, f32[1,1,16,6144]{3,2,1,0:T(8,128)}, f32[1,1,16,6144]{3,2,1,0:T(8,128)}, f32[1,1,16,6144]{3,2,1,0:T(8,128)}) custom-call(bf16[512,6144]{1,0:T(8,128)(2,1)S(1)} %get-tuple-element.12.refs_0_, f32[1,1,16,6144]{3,2,1,0:T(8,128)S(1)} %get-tuple-element.13.refs_1_, ...), custom_call_target="tpu_custom_call" | custom-call | tf_op jit(solution)/shard_map/pallas_call | solution.py:411

commit v4 on v3

v4 whole, which is shorter than its diff:
```python
import functools

import jax
import jax.numpy as jnp
from jax import lax
from jax.experimental import pallas as pl
from jax.experimental.pallas import tpu as pltpu
from jax.sharding import Mesh
from jax.sharding import PartitionSpec as P

MESH = pl.DeviceIdType.MESH
BF16, F32 = jnp.bfloat16, jnp.float32
N = 4
WR = 512
WG = 512
TILE = 256
WU = 512
RS_LAG = (6, 6, 6)
AG_LAG = (6, 6, 2)


def main_kernel(
    sizes, order_in, steps_in, max_rms_in, grad, master, first, second,
    out, new_master, new_first, new_second,
    own, sib, sb, hop, fin, s2, r2, tot, gsum, slots, perm, perm_t, st, fix, sq, s1, s2nd, order, steps, max_rms,
    load_sem, pair_sem, hop_sem, fin_sem, r2_sem, tot_sem, st_sem, x_sem, yz_sem, p1_sem, p2_sem, fwd_sem, half_sem, small_sem, met_sem,
):
    rows, width, nr, ng, entries = sizes
    my, mz, mc, mx = (lax.axis_index(a) for a in "yzcx")
    half = width // 2
    coords = {"y": my, "z": mz}
    ring = {a: [lax.rem(lax.axis_index(a) + d, N) for d in range(N)] for a in "yzx"}

    def device(y=my, z=mz, c=mc, x=mx):
        return y, z, c, x

    at = {a: [device(**{a: ring[a][d]}) for d in range(N)] for a in "yzx"}
    sibling = device(c=1 - mc)

    def axes(block):
        return ("y", "z") if block % 2 == 0 else ("z", "y")

    def send(src, dst, sems, n, where):
        pltpu.make_async_remote_copy(
            src_ref=src, dst_ref=dst, send_sem=sems.at[0], recv_sem=sems.at[1 + n],
            device_id=where, device_id_type=MESH,
        ).start()

    def wait(ref, sem):
        pltpu.make_async_remote_copy(
            src_ref=ref, dst_ref=ref, send_sem=sem, recv_sem=sem,
            device_id=sibling, device_id_type=MESH,
        ).wait_recv()

    def load(k):
        cols = pl.ds(pl.multiple_of(mc * half + k * WR, WR), WR)
        return pltpu.make_async_copy(grad.at[0, :, cols], own.at[k], load_sem.at[k])

    loads = [load(k) for k in range(nr)]
    states = [
        pltpu.make_async_copy(a.at[0, 0], st.at[i], st_sem.at[i])
        for i, a in enumerate((master, first, second))
    ]
    small = [
        pltpu.make_async_copy(a, b, small_sem.at[i])
        for i, (a, b) in enumerate(((order_in, order), (steps_in, steps), (max_rms_in, max_rms)))
    ]
    for c in [*small, *loads, *states]:
        c.start()

    peers_x = [device(x=ring["x"][i], c=c) for i in range(N) for c in (mc, 1 - mc)][1:]
    peers_yz = [device(y=ring["y"][i], z=ring["z"][j]) for i in range(N) for j in range(N)][1:]

    def signal(sem, where):
        pl.semaphore_signal(sem, inc=1, device_id=where, device_id_type=MESH)

    beside_x = [at["x"][1], at["x"][3]]
    nearest = [sibling, *(at[a][d] for a in "yz" for d in (1, 3)), *beside_x]
    barrier = pltpu.get_barrier_semaphore()
    for peer in nearest:
        signal(barrier, peer)

    def fill(t, _):
        i = lax.broadcasted_iota(jnp.int32, (16, rows), 0)
        picked = jnp.zeros((16, rows), jnp.int32)
        for b in range(8):
            picked = jnp.where(i // 2 == b, order[t * 8 + b] * 2, picked)
        hit = lax.broadcasted_iota(jnp.int32, (16, rows), 1) == picked + i % 2
        perm[pl.ds(pl.multiple_of(t * 16, 16), 16), :] = jnp.where(hit, 1.0, 0.0).astype(BF16)
        return 0

    small[0].wait()
    lax.fori_loop(0, rows // 16, fill, 0)
    pl.semaphore_wait(barrier, len(nearest))

    for k in range(nr):
        cols = pl.ds(pl.multiple_of((1 - mc) * half + k * WR, WR), WR)
        send(grad.at[0, :, cols], sib.at[k], pair_sem, k, sibling)
    for peer in beside_x:
        signal(met_sem.at[0], peer)

    def pick_rows(k):
        loads[k].wait()
        wait(sib.at[k], pair_sem.at[1 + k])
        for t in range(WR // TILE):
            cols = pl.ds(t * TILE, TILE)
            both = own[k, :, cols].astype(F32) + sib[k, :, cols].astype(F32)
            moved = jnp.dot(perm[...], both.astype(BF16), preferred_element_type=F32)
            moved = moved.astype(BF16).reshape(N, N, 32, TILE)
            for i in range(N):
                for j in range(N):
                    at = (i, j) if k % 2 == 0 else (j, i)
                    sb[k, at[0], at[1], :, cols] = moved[i, j]

    lo, hi = pl.ds(0, 2), pl.ds(2, 2)

    def first_hops(k):
        a = axes(k)[0]
        _, up, far, down = ring[a]
        send(sb.at[k, far, lo], hop.at[k, 0], hop_sem, k, at[a][1])
        send(sb.at[k, far, hi], hop.at[k, 1], hop_sem, k, at[a][3])
        send(sb.at[k, up, hi], fin.at[k, 0, hi], fin_sem, k, at[a][1])
        send(sb.at[k, down, lo], fin.at[k, 1, lo], fin_sem, k, at[a][3])

    def second_hops(k):
        a = axes(k)[0]
        _, up, _, down = ring[a]
        wait(hop.at[k], hop_sem.at[1 + k])
        for slot, to, part in ((0, up, lo), (1, down, hi)):

            def body(i, _, slot=slot, to=to):
                r = pl.ds(pl.multiple_of(i * 16, 16), 16)
                for j in range(2):
                    mine = sb[k, to, 2 * slot + j, r, :].astype(F32)
                    sb[k, to, 2 * slot + j, r, :] = (mine + hop[k, slot, j, r, :].astype(F32)).astype(BF16)
                return 0

            lax.fori_loop(0, 2, body, 0)
            send(sb.at[k, to, part], fin.at[k, slot, part], fin_sem, k, at[a][1 + 2 * slot])

    def sum3(k, me, j, r):
        return sb[k, me, j, r, :].astype(F32) + fin[k, 0, j, r, :].astype(F32) + fin[k, 1, j, r, :].astype(F32)

    def across(k):
        a, b = axes(k)
        me = coords[a]
        wait(fin.at[k], fin_sem.at[1 + k])
        for d in (2, 1, 3):
            j = ring[b][d]

            def body(i, _, j=j, d=d):
                r = pl.ds(pl.multiple_of(i * 16, 16), 16)
                s2[k, d - 1, r, :] = sum3(k, me, j, r).astype(BF16)
                return 0

            lax.fori_loop(0, 2, body, 0)
            send(s2.at[k, d - 1], r2.at[k, d - 1], r2_sem, k, at[b][d])

    def finish(k):
        a, b = axes(k)
        me, mj = coords[a], coords[b]
        wait(r2.at[k], r2_sem.at[1 + k])
        cols = pl.ds(pl.multiple_of(mc * half + k * WR, WR), WR)
        for i in range(2):
            r = pl.ds(i * 16, 16)
            total = sum3(k, me, mj, r)
            for d in range(3):
                total = total + r2[k, d, r, :].astype(F32)
            tot[k, i] = total
            square = total * total
            folded = square[:, :128]
            for t in range(1, WR // 128):
                folded = folded + square[:, t * 128 : (t + 1) * 128]
            sq[...] += folded[:8] + folded[8:]
        gsum[:, cols] = tot[k, mc]
        send(tot.at[k, 1 - mc], gsum.at[:, cols], tot_sem, 0, sibling)

    sq[...] = jnp.zeros_like(sq)
    for t in range(nr + sum(RS_LAG)):
        if t < nr:
            pick_rows(t)
            first_hops(t)
        k = t - RS_LAG[0]
        if 0 <= k < nr:
            second_hops(k)
        k -= RS_LAG[1]
        if k == 0:
            pl.semaphore_wait(met_sem.at[0], 2)
            for peer in beside_x:
                signal(met_sem.at[1], peer)
        if 0 <= k < nr:
            across(k)
        k -= RS_LAG[2]
        if 0 <= k < nr:
            finish(k)

    mine_x, mine_yz = mx * 2 + mc, my * N + mz
    s1[mine_x] = sq[...]
    pl.semaphore_wait(met_sem.at[1], 2)
    for peer in peers_x:
        send(sq, s1.at[mine_x], x_sem, 0, peer)

    def flip(t, _):
        r = pl.ds(pl.multiple_of(t * 128, 128), 128)
        i = lax.broadcasted_iota(jnp.int32, (128, rows), 0) + t * 128
        eye = jnp.where(i == lax.broadcasted_iota(jnp.int32, (128, rows), 1), 1.0, 0.0).astype(BF16)
        perm_t[r, :] = lax.dot_general(
            eye, perm[...], (((1,), (1,)), ((), ())), preferred_element_type=F32
        ).astype(BF16)
        return 0

    lax.fori_loop(0, rows // 128, flip, 0)
    small[1].wait()
    small[2].wait()
    lane_row = lax.broadcasted_iota(jnp.int32, (16, WU), 0)
    count = jnp.zeros((16, WU), jnp.int32)
    for i in range(16):
        count = jnp.where(lane_row == i, steps[0, 0, i], count)
    count = count.astype(F32)
    fix[0] = 1.0 - jnp.power(jnp.full((16, WU), 0.9, F32), count)
    fix[1] = 1.0 - jnp.power(jnp.full((16, WU), 0.95, F32), count)
    for c in states:
        c.wait()

    for ref, sems in ((sib, pair_sem), (hop, hop_sem), (fin, fin_sem), (r2, r2_sem)):
        wait(ref, sems.at[0])

    few = s1.at[pl.ds(0, len(peers_x))]
    many = s2nd.at[pl.ds(0, len(peers_yz))]
    wait(few, x_sem.at[1])
    part = s1[0]
    for i in range(1, 2 * N):
        part = part + s1[i]
    s2nd[mine_yz] = part
    mine = s2nd.at[mine_yz]
    for peer in peers_yz:
        send(mine, mine, yz_sem, 0, peer)
    given = gsum.at[:, pl.ds(0, half)]
    wait(few, x_sem.at[0])
    wait(given, tot_sem.at[0])
    wait(given, tot_sem.at[1])
    wait(many, yz_sem.at[1])
    part = s2nd[0]
    for i in range(1, N * N):
        part = part + s2nd[i]
    square_sum = jnp.sum(jnp.sum(part, axis=1, keepdims=True), axis=0, keepdims=True)
    clip = jnp.minimum(1.0, max_rms[0] / jnp.sqrt(square_sum / entries + 1e-06))

    def update(k):
        def body(t, _):
            cols = pl.ds(pl.multiple_of(k * WG + t * WU, WU), WU)
            clipped = clip * gsum[:, cols]
            moment = 0.9 * st[1, :, cols] + 0.1 * clipped
            variance = 0.95 * st[2, :, cols] + 0.05 * clipped * clipped
            ratio = moment / fix[0] / (jnp.sqrt(variance / fix[1]) + 1e-08)
            old = st[0, :, cols]
            fresh = old - 0.1 * (ratio + 0.1 * old)
            new_master[0, 0, :, cols] = fresh
            new_first[0, 0, :, cols] = moment
            new_second[0, 0, :, cols] = variance
            slots[my, mz, mc, :, cols] = fresh.astype(BF16)
            return 0

        lax.fori_loop(0, WG // WU, body, 0)
        cols = pl.ds(k * WG, WG)
        a = axes(k)[0]
        mine = slots.at[my, mz, mc, :, cols]
        for d in (2, 1, 3):
            send(mine, mine, p1_sem, k, at[a][d])

    def row(k, at, part):
        cols = pl.ds(k * WG, WG)
        if k % 2 == 0:
            return slots.at[part, at, mc, :, cols]
        return slots.at[at, part, mc, :, cols]

    def spread(k):
        b = axes(k)[1]
        wait(slots.at[0, pl.ds(0, 3), 0, :, pl.ds(k * WG, WG)], p1_sem.at[1 + k])
        mine = row(k, coords[b], pl.ds(0, N))
        for d in (1, 3):
            send(mine, mine, p2_sem, k, at[b][d])

    def forward(k):
        b = axes(k)[1]
        wait(slots.at[pl.ds(0, 2), :, 0, :, pl.ds(k * WG, WG)], p2_sem.at[1 + k])
        for d, part in ((1, lo), (3, hi)):
            block = row(k, ring[b][4 - d], part)
            send(block, block, fwd_sem, k, at[b][d])

    def to_sibling(k):
        wait(slots.at[0, :, 0, :, pl.ds(k * WG, WG)], fwd_sem.at[1 + k])
        block = slots.at[:, :, mc, :, pl.ds(k * WG, WG)]
        send(block, block, half_sem, k, sibling)

    def put_back(k):
        wait(slots.at[:, :, 0, :, pl.ds(k * WG, WG)], half_sem.at[1 + k])
        for t in range(WG // TILE):
            cols = pl.ds(k * WG + t * TILE, TILE)
            block = slots[:, :, :, :, cols].reshape(rows, TILE)
            out[:, cols] = jnp.dot(perm_t[...], block, preferred_element_type=F32).astype(BF16)

    for k in range(ng):
        update(k)
    for t in range(ng + sum(AG_LAG)):
        if t < ng:
            spread(t)
        k = t - AG_LAG[0]
        if 0 <= k < ng:
            forward(k)
        k -= AG_LAG[1]
        if 0 <= k < ng:
            to_sibling(k)
        k -= AG_LAG[2]
        if 0 <= k < ng:
            put_back(k)
    wait(many, yz_sem.at[0])
    wait(slots.at[0, pl.ds(0, 3), 0], p1_sem.at[0])
    wait(slots.at[pl.ds(0, 2), :, 0], p2_sem.at[0])
    wait(slots.at[0, :, 0], fwd_sem.at[0])
    wait(slots.at[:, :, 0], half_sem.at[0])


def write_kernel(*refs):
    n = (len(refs) - 1) // 2
    sem = refs[2 * n]
    copies = [
        pltpu.make_async_copy(refs[0].at[pl.ds(i * 64, 64)], refs[n].at[pl.ds(i * 64, 64)], sem.at[i])
        for i in range(8)
    ]
    copies += [
        pltpu.make_async_copy(refs[i], refs[n + i], sem.at[7 + i]) for i in range(1, n)
    ]
    for c in copies:
        c.start()
    for c in copies:
        c.wait()


def shards(grad_parts, bucket_order, master, first_moment, second_moment, step_count, max_rms):
    _, rows, width = grad_parts.shape
    own_rows = master.shape[2]
    nr, ng = width // 2 // WR, width // WG
    entries = float(rows * width * lax.axis_size("x"))
    dma = pltpu.SemaphoreType.DMA
    anywhere = pl.BlockSpec(memory_space=pl.ANY)
    vmem = pl.BlockSpec(memory_space=pltpu.VMEM)
    state = pltpu.VMEM(master.shape, F32)
    results = pl.pallas_call(
        functools.partial(main_kernel, (rows, width, nr, ng, entries)),
        out_shape=(pltpu.VMEM((rows, width), BF16), state, state, state),
        in_specs=[pl.BlockSpec(memory_space=pltpu.HBM)] * 7,
        out_specs=[vmem] * 4,
        scratch_shapes=[
            pltpu.VMEM((nr, rows, WR), BF16),
            pltpu.VMEM((nr, rows, WR), BF16),
            pltpu.VMEM((nr, N, N, 32, WR), BF16),
            pltpu.VMEM((nr, 2, 2, 32, WR), BF16),
            pltpu.VMEM((nr, 2, N, 32, WR), BF16),
            pltpu.VMEM((nr, 3, 32, WR), BF16),
            pltpu.VMEM((nr, 3, 32, WR), BF16),
            pltpu.VMEM((nr, 2, 16, WR), F32),
            pltpu.VMEM((own_rows, width), F32),
            pltpu.VMEM((N, N, 2, own_rows, width), BF16),
            pltpu.VMEM((rows, rows), BF16),
            pltpu.VMEM((rows, rows), BF16),
            pltpu.VMEM((3, own_rows, width), F32),
            pltpu.VMEM((2, own_rows, WU), F32),
            pltpu.VMEM((8, 128), F32),
            pltpu.VMEM((2 * N, 8, 128), F32),
            pltpu.VMEM((N * N, 8, 128), F32),
            pltpu.SMEM(bucket_order.shape, jnp.int32),
            pltpu.SMEM(step_count.shape, jnp.int32),
            pltpu.SMEM(max_rms.shape, F32),
            dma((nr,)),
            *[dma((1 + nr,))] * 4,
            dma((2,)),
            dma((3,)),
            *[dma((2,))] * 2,
            *[dma((1 + ng,))] * 4,
            dma((3,)),
            pltpu.SemaphoreType.REGULAR((2,)),
        ],
        compiler_params=pltpu.CompilerParams(
            collective_id=0, has_side_effects=True, vmem_limit_bytes=48 << 20
        ),
    )(bucket_order, step_count, max_rms, grad_parts, master, first_moment, second_moment)
    fresh, *moved = pl.pallas_call(
        write_kernel,
        out_shape=[jax.ShapeDtypeStruct(r.shape, r.dtype) for r in results],
        in_specs=[anywhere] * 4,
        out_specs=[pl.BlockSpec(memory_space=pltpu.HBM)] * 4,
        scratch_shapes=[dma((11,))],
        compiler_params=pltpu.CompilerParams(vmem_limit_bytes=1 << 20),
    )(*(pltpu.with_memory_space_constraint(r, pltpu.VMEM) for r in results))
    return (*moved, fresh)


def solution(mesh):
    dp = ("y", "z", "c")
    finer = Mesh(mesh.devices.reshape(N, N, 2, mesh.shape["expert"]), (*dp, "x"))
    state = P("x", dp, None, None)
    return jax.shard_map(
        shards,
        mesh=finer,
        in_specs=(P(dp, "x", None), P(), state, state, state, P("x", dp, None), P()),
        out_specs=(state, state, state, P("x", None)),
        check_vma=False,
    )
```

time: 71.6 us -> 67.3 us (0.940)
  Pallas kernels: 70.2 us -> 65.9 us
    pallas_call x1, Pallas kernels: 67.1 us -> 62.8 us  [shards(): pl.pallas_call(functools.partial(main_kernel, (rows, width, nr, ng, entri...]
where the time goes in v4:
time: 67.3 us; the launch traced here: 67.2 us
  Pallas kernels  65.9 us (98%)
  between operations  1.29 us (2%)
    pallas_call x1, Pallas kernels, shards(): pl.pallas_call(functools.partial(main_kernel, (rows, width, nr, ng, entri...  62.8 us
    pallas_call x1, Pallas kernels, shards(): pl.pallas_call(write_kernel, out_shape=[jax.ShapeDtypeStruct(r.shape, r.d...  3.11 us

profile of v4, /device:TPU:1, one launch (start us, length us, event | category | flops | bytes accessed | tf_op | source)
XLA Modules:
  0.0 67.2 jit_solution(7716418753272278693)
XLA Ops:
  1.3 62.8 %shard_map.102 = (bf16[512,6144]{1,0:T(8,128)(2,1)S(1)}, f32[1,1,16,6144]{3,2,1,0:T(8,128)S(1)}, f32[1,1,16,6144]{3,2,1,0:T(8,128)S(1)}, f32[1,1,16,6144]{3,2,1,0:T(8,128)S(1)}) custom-call(s32[256]{0:T(256)} %order_in.1, s32[1,1,16]{2,1,0:T(1,128)} %steps_in.1, f32[1]{0:T(128)S(6)} %copy.11.max_rms_in, bf16[1,512,6144]{2,1,0:T(8,128)(2,1)} %grad.1, ...), custom_call_target="tpu_custom_call" | custom-call | tf_op jit(solution)/shard_map/pallas_call | solution.py:349
  64.1 3.1 %shard_map.103 = (bf16[512,6144]{1,0:T(8,128)(2,1)}, f32[1,1,16,6144]{3,2,1,0:T(8,128)}, f32[1,1,16,6144]{3,2,1,0:T(8,128)}, f32[1,1,16,6144]{3,2,1,0:T(8,128)}) custom-call(bf16[512,6144]{1,0:T(8,128)(2,1)S(1)} %get-tuple-element.12.refs_0_, f32[1,1,16,6144]{3,2,1,0:T(8,128)S(1)} %get-tuple-element.13.refs_1_, ...), custom_call_target="tpu_custom_call" | custom-call | tf_op jit(solution)/shard_map/pallas_call | solution.py:388

commit v5 on v4

--- a/solution.py
+++ b/solution.py
@@ -17,12 +17,21 @@
 WU = 512
 RS_LAG = (6, 6, 6)
 AG_LAG = (6, 6, 2)
+LATE = 6
+
+
+def restore(slots, perm_t, out, start, to):
+    rows = perm_t.shape[0]
+    for t in range(WG // TILE):
+        block = slots[:, :, :, :, pl.ds(start + t * TILE, TILE)].reshape(rows, TILE)
+        moved = jnp.dot(perm_t[...], block, preferred_element_type=F32)
+        out[:, pl.ds(to + t * TILE, TILE)] = moved.astype(BF16)
 
 
 def main_kernel(
     sizes, order_in, steps_in, max_rms_in, grad, master, first, second,
-    out, new_master, new_first, new_second,
-    own, sib, sb, hop, fin, s2, r2, tot, gsum, slots, perm, perm_t, st, fix, sq, s1, s2nd, order, steps, max_rms,
+    out, new_master, new_first, new_second, slots, perm_t,
+    own, sib, sb, hop, fin, s2, r2, tot, gsum, perm, st, fix, sq, s1, s2nd, order, steps, max_rms,
     load_sem, pair_sem, hop_sem, fin_sem, r2_sem, tot_sem, st_sem, x_sem, yz_sem, p1_sem, p2_sem, fwd_sem, half_sem, small_sem, met_sem,
 ):
     rows, width, nr, ng, entries = sizes
@@ -176,23 +185,23 @@
         send(tot.at[k, 1 - mc], gsum.at[:, cols], tot_sem, 0, sibling)
 
     sq[...] = jnp.zeros_like(sq)
+    def meet():
+        pl.semaphore_wait(met_sem.at[0], 2)
+        for peer in beside_x:
+            signal(met_sem.at[1], peer)
+
+    def pick_and_send(k):
+        pick_rows(k)
+        first_hops(k)
+
     for t in range(nr + sum(RS_LAG)):
-        if t < nr:
-            pick_rows(t)
-            first_hops(t)
-        k = t - RS_LAG[0]
-        if 0 <= k < nr:
-            second_hops(k)
-        k -= RS_LAG[1]
-        if k == 0:
-            pl.semaphore_wait(met_sem.at[0], 2)
-            for peer in beside_x:
-                signal(met_sem.at[1], peer)
-        if 0 <= k < nr:
-            across(k)
-        k -= RS_LAG[2]
-        if 0 <= k < nr:
-            finish(k)
+        if t == RS_LAG[0]:
+            meet()
+        k = t
+        for lag, stage in zip((0, *RS_LAG), (pick_and_send, second_hops, across, finish), strict=True):
+            k -= lag
+            if 0 <= k < nr:
+                stage(k)
 
     mine_x, mine_yz = mx * 2 + mc, my * N + mz
     s1[mine_x] = sq[...]
@@ -295,25 +304,18 @@
 
     def put_back(k):
         wait(slots.at[:, :, 0, :, pl.ds(k * WG, WG)], half_sem.at[1 + k])
-        for t in range(WG // TILE):
-            cols = pl.ds(k * WG + t * TILE, TILE)
-            block = slots[:, :, :, :, cols].reshape(rows, TILE)
-            out[:, cols] = jnp.dot(perm_t[...], block, preferred_element_type=F32).astype(BF16)
+        restore(slots, perm_t, out, k * WG, k * WG)
 
     for k in range(ng):
         update(k)
     for t in range(ng + sum(AG_LAG)):
-        if t < ng:
-            spread(t)
-        k = t - AG_LAG[0]
-        if 0 <= k < ng:
-            forward(k)
-        k -= AG_LAG[1]
-        if 0 <= k < ng:
-            to_sibling(k)
-        k -= AG_LAG[2]
-        if 0 <= k < ng:
-            put_back(k)
+        k = t
+        for lag, stage in zip((0, *AG_LAG), (spread, forward, to_sibling, put_back), strict=True):
+            k -= lag
+            if 0 <= k < (ng - LATE if stage is put_back else ng):
+                stage(k)
+    for k in range(ng - LATE, ng):
+        wait(slots.at[:, :, 0, :, pl.ds(k * WG, WG)], half_sem.at[1 + k])
     wait(many, yz_sem.at[0])
     wait(slots.at[0, pl.ds(0, 3), 0], p1_sem.at[0])
     wait(slots.at[pl.ds(0, 2), :, 0], p2_sem.at[0])
@@ -321,18 +323,21 @@
     wait(slots.at[:, :, 0], half_sem.at[0])
 
 
-def write_kernel(*refs):
-    n = (len(refs) - 1) // 2
-    sem = refs[2 * n]
+def write_kernel(ready, m0, m1, m2, slots, perm_t, out, o0, o1, o2, tail, sem):
+    first = ready.shape[1]
     copies = [
-        pltpu.make_async_copy(refs[0].at[pl.ds(i * 64, 64)], refs[n].at[pl.ds(i * 64, 64)], sem.at[i])
-        for i in range(8)
-    ]
-    copies += [
-        pltpu.make_async_copy(refs[i], refs[n + i], sem.at[7 + i]) for i in range(1, n)
+        pltpu.make_async_copy(src, dst, sem.at[i])
+        for i, (src, dst) in enumerate(((ready, out.at[:, pl.ds(0, first)]), (m0, o0), (m1, o1), (m2, o2)))
     ]
     for c in copies:
         c.start()
+    for k in range(LATE):
+        restore(slots, perm_t, tail, first + k * WG, k * WG)
+        part = pltpu.make_async_copy(
+            tail.at[:, pl.ds(k * WG, WG)], out.at[:, pl.ds(first + k * WG, WG)], sem.at[4 + k]
+        )
+        part.start()
+        copies.append(part)
     for c in copies:
         c.wait()
 
@@ -343,14 +348,20 @@
     nr, ng = width // 2 // WR, width // WG
     entries = float(rows * width * lax.axis_size("x"))
     dma = pltpu.SemaphoreType.DMA
-    anywhere = pl.BlockSpec(memory_space=pl.ANY)
     vmem = pl.BlockSpec(memory_space=pltpu.VMEM)
     state = pltpu.VMEM(master.shape, F32)
     results = pl.pallas_call(
         functools.partial(main_kernel, (rows, width, nr, ng, entries)),
-        out_shape=(pltpu.VMEM((rows, width), BF16), state, state, state),
+        out_shape=(
+            pltpu.VMEM((rows, width - LATE * WG), BF16),
+            state,
+            state,
+            state,
+            pltpu.VMEM((N, N, 2, own_rows, width), BF16),
+            pltpu.VMEM((rows, rows), BF16),
+        ),
         in_specs=[pl.BlockSpec(memory_space=pltpu.HBM)] * 7,
-        out_specs=[vmem] * 4,
+        out_specs=[vmem] * 6,
         scratch_shapes=[
             pltpu.VMEM((nr, rows, WR), BF16),
             pltpu.VMEM((nr, rows, WR), BF16),
@@ -361,8 +372,6 @@
             pltpu.VMEM((nr, 3, 32, WR), BF16),
             pltpu.VMEM((nr, 2, 16, WR), F32),
             pltpu.VMEM((own_rows, width), F32),
-            pltpu.VMEM((N, N, 2, own_rows, width), BF16),
-            pltpu.VMEM((rows, rows), BF16),
             pltpu.VMEM((rows, rows), BF16),
             pltpu.VMEM((3, own_rows, width), F32),
             pltpu.VMEM((2, own_rows, WU), F32),
@@ -387,11 +396,14 @@
     )(bucket_order, step_count, max_rms, grad_parts, master, first_moment, second_moment)
     fresh, *moved = pl.pallas_call(
         write_kernel,
-        out_shape=[jax.ShapeDtypeStruct(r.shape, r.dtype) for r in results],
-        in_specs=[anywhere] * 4,
+        out_shape=[
+            jax.ShapeDtypeStruct((rows, width), BF16),
+            *[jax.ShapeDtypeStruct(master.shape, F32)] * 3,
+        ],
+        in_specs=[vmem] * 6,
         out_specs=[pl.BlockSpec(memory_space=pltpu.HBM)] * 4,
-        scratch_shapes=[dma((11,))],
-        compiler_params=pltpu.CompilerParams(vmem_limit_bytes=1 << 20),
+        scratch_shapes=[pltpu.VMEM((rows, LATE * WG), BF16), dma((4 + LATE,))],
+        compiler_params=pltpu.CompilerParams(vmem_limit_bytes=12 << 20),
     )(*(pltpu.with_memory_space_constraint(r, pltpu.VMEM) for r in results))
     return (*moved, fresh)
 

time: 67.3 us -> 66.8 us (level)
  no operation moved by 1% of the time
where the time goes in v5:
time: 66.8 us; the launch traced here: 66.6 us
  Pallas kernels  65.3 us (98%)
  between operations  1.29 us (2%)
    pallas_call x1, Pallas kernels, shards(): pl.pallas_call(functools.partial(main_kernel, (rows, width, nr, ng, entri...  62.2 us
    pallas_call x1, Pallas kernels, shards(): pl.pallas_call(write_kernel, out_shape=[jax.ShapeDtypeStruct((rows, width...  3.12 us

profile of v5, /device:TPU:1, one launch (start us, length us, event | category | flops | bytes accessed | tf_op | source)
XLA Modules:
  0.0 66.6 jit_solution(7714412625660594280)
XLA Ops:
  1.3 62.2 %shard_map.102 = (bf16[512,3072]{1,0:T(8,128)(2,1)S(1)}, f32[1,1,16,6144]{3,2,1,0:T(8,128)S(1)}, f32[1,1,16,6144]{3,2,1,0:T(8,128)S(1)}, f32[1,1,16,6144]{3,2,1,...) custom-call(s32[256]{0:T(256)} %order_in.1, s32[1,1,16]{2,1,0:T(1,128)} %steps_in.1, ...), custom_call_target="tpu_custom_call" | custom-call | tf_op jit(solution)/shard_map/pallas_call | solution.py:353
  63.5 3.1 %shard_map.103 = (bf16[512,6144]{1,0:T(8,128)(2,1)}, f32[1,1,16,6144]{3,2,1,0:T(8,128)}, f32[1,1,16,6144]{3,2,1,0:T(8,128)}, f32[1,1,16,6144]{3,2,1,0:T(8,128)}) custom-call(bf16[512,3072]{1,0:T(8,128)(2,1)S(1)} %get-tuple-element.14.ready, f32[1,1,16,6144]{3,2,1,0:T(8,128)S(1)} %get-tuple-element.15.m0, f32[1,1,16,6144]{3,2,1,0:T(8,128)S(1)} %get-tuple-element.16.m1, ...), custom_call_target="tpu_custom_call" | custom-call | tf_op jit(solution)/shard_map/pallas_call | solution.py:397
